TPU v7x, 256 devices: a whole 4x4x8 slice. The times are simulated.
256 devices in a mesh: outer: 32 (over z, x), inner: 8 (over y, core).
Axes of the slice: x: 4, y: 4, z: 8, core: 2. Of those that a mesh axis runs over, the one named last changes fastest.
Arguments:
- queries: bfloat16 [32768, 2048], P(('outer', 'inner')), may hold values from -5 to 5
- key_rows: bfloat16 [32768, 2048], P(('outer', 'inner')), may hold values from -5 to 5
- value_rows: bfloat16 [32768, 2048], P(('outer', 'inner')), may hold values from -6 to 6
- out_grad: bfloat16 [32768, 2048], P(('outer', 'inner')), may hold values from -6 to 6
- log_gate: float32 [16, 32768], P(None, ('outer', 'inner')), may hold values from -1 to 0
Outputs:
- mixed_out: bfloat16 [32768, 2048], P(('outer', 'inner'))
- query_grad: bfloat16 [32768, 2048], P(('outer', 'inner'))
- key_grad: bfloat16 [32768, 2048], P(('outer', 'inner'))
- value_grad: bfloat16 [32768, 2048], P(('outer', 'inner'))
All inputs are finite; a program needn't handle non-finite values.
Results may differ from a plain program's by a relative error of at most 0.007.
Values may be sent and summed in bfloat16 or wider, within the bound.
No kernel may reach another device: no remote copies, remote signals or barrier semaphores. Data moves between devices by JAX's collectives and lax.ppermute only.
A program may use at most 256 MiB of HBM per device.

v0:
```python
import jax
import jax.numpy as jnp
from jax import lax
from jax.sharding import PartitionSpec as P

W = 64


def from_behind(value, axis, steps):
    count = lax.axis_size(axis)
    first, last = (max(0, -steps), min(count, count - steps))
    return lax.ppermute(value, axis, [(source, source + steps) for source in range(first, last)])


def carried_in(part, axis, combine, identity, reverse):
    count = lax.axis_size(axis)
    place = lax.axis_index(axis)
    ahead = count - 1 - place if reverse else place
    gathered = jax.tree.map(lambda a: lax.all_gather(a, axis), part)
    state = jax.tree.map(lambda a, e: jnp.zeros_like(a) + jnp.asarray(e, a.dtype), part, identity)

    def one(hop, state):
        source = count - 1 - hop if reverse else hop
        return combine(
            state, jax.tree.map(lambda a: lax.dynamic_index_in_dim(a, source, 0, False), gathered)
        )

    return lax.fori_loop(0, ahead, one, state)


def low_product(form, left, right):
    return jnp.einsum(form, left, right, preferred_element_type=jnp.float32)


def high_product(form, left, right):
    return jnp.einsum(form, left, right, precision=lax.Precision.HIGHEST)


def local_states(query_blk, key_blk, value_blk, grad_blk, gate_rows):
    cumul_gate = jnp.cumsum(gate_rows, axis=1)
    last_cumul = cumul_gate[:, -1:]
    block_decay = jnp.exp(cumul_gate[:, -1])
    tail_weight = jnp.exp(last_cumul - cumul_gate).T
    head_weight = jnp.exp(cumul_gate).T
    state_local = high_product(
        "thf,the->hfe",
        key_blk.astype(jnp.float32) * tail_weight[:, :, None],
        value_blk.astype(jnp.float32),
    )
    grad_local = high_product(
        "thf,the->hfe",
        query_blk.astype(jnp.float32) * head_weight[:, :, None],
        grad_blk.astype(jnp.float32),
    )
    return (block_decay, state_local, grad_local)


def block_terms(
    query_blk,
    key_blk,
    value_blk,
    grad_blk,
    gate_rows,
    state_in,
    grad_after,
    key_halo,
    value_halo,
    halo_live,
    lin_scale,
):
    row_count = query_blk.shape[0]
    halo_rows = key_halo.shape[0]
    head_size = query_blk.shape[2]
    cumul_gate = jnp.cumsum(gate_rows, axis=1)
    last_cumul = cumul_gate[:, -1:]
    head_weight = jnp.exp(cumul_gate).T
    tail_weight = jnp.exp(last_cumul - cumul_gate).T
    query_pos = jnp.arange(row_count)[:, None]
    key_pos = jnp.arange(row_count)[None, :]
    causal_mask = (key_pos <= query_pos)[None]
    gap_logs = cumul_gate[:, :, None] - cumul_gate[:, None, :]
    decay_grid = jnp.where(causal_mask, jnp.exp(jnp.where(causal_mask, gap_logs, 0.0)), 0.0)
    lin_weight = (low_product("thf,shf->hts", query_blk, key_blk) * decay_grid).astype(jnp.bfloat16)
    query_decayed = query_blk.astype(jnp.float32) * head_weight[:, :, None]
    lin_out = low_product("hts,she->the", lin_weight, value_blk) + high_product(
        "thf,hfe->the", query_decayed, state_in
    )
    ext_keys = jnp.concatenate([key_halo, key_blk], axis=0)
    ext_values = jnp.concatenate([value_halo, value_blk], axis=0)
    ext_pos = jnp.arange(row_count + halo_rows)[None, :]
    in_band = (
        (ext_pos > query_pos)
        & (ext_pos <= query_pos + halo_rows)
        & ((ext_pos >= halo_rows) | halo_live)
    )[None]
    logits = low_product("thf,jhf->htj", query_blk, ext_keys) * head_size ** (-0.5)
    masked_logits = jnp.where(in_band, logits, -jnp.inf)
    row_max = jnp.max(masked_logits, axis=2, keepdims=True)
    expo_terms = jnp.exp(masked_logits - row_max)
    win_prob = expo_terms / jnp.sum(expo_terms, axis=2, keepdims=True)
    prob_low = win_prob.astype(jnp.bfloat16)
    win_out = low_product("htj,jhe->the", prob_low, ext_values)
    output = (lin_scale * lin_out + win_out).astype(jnp.bfloat16)
    grad_weight = (low_product("the,she->hts", grad_blk, value_blk) * decay_grid).astype(
        jnp.bfloat16
    )
    grad_decayed = grad_blk.astype(jnp.float32) * head_weight[:, :, None]
    query_lin = low_product("hts,shf->thf", grad_weight, key_blk) + high_product(
        "the,hfe->thf", grad_decayed, state_in
    )
    value_tail = value_blk.astype(jnp.float32) * tail_weight[:, :, None]
    key_tail = key_blk.astype(jnp.float32) * tail_weight[:, :, None]
    key_lin = low_product("hts,thf->shf", grad_weight, query_blk) + high_product(
        "she,hfe->shf", value_tail, grad_after
    )
    value_lin = low_product("hts,the->she", lin_weight, grad_blk) + high_product(
        "shf,hfe->she", key_tail, grad_after
    )
    prob_grad = low_product("the,jhe->htj", grad_blk, ext_values)
    row_delta = jnp.sum(win_prob * prob_grad, axis=2, keepdims=True)
    logit_grad = (win_prob * (prob_grad - row_delta) * head_size ** (-0.5)).astype(jnp.bfloat16)
    query_win = low_product("htj,jhf->thf", logit_grad, ext_keys)
    key_ext = low_product("htj,thf->jhf", logit_grad, query_blk)
    value_ext = low_product("htj,the->jhe", prob_low, grad_blk)
    query_grad = (lin_scale * query_lin + query_win).astype(jnp.bfloat16)
    key_local = lin_scale * key_lin + key_ext[halo_rows:]
    value_local = lin_scale * value_lin + value_ext[halo_rows:]
    return (output, query_grad, key_local, value_local, key_ext[:halo_rows], value_ext[:halo_rows])


def forward_merge(earlier_part, later_part):
    return (
        earlier_part[0] * later_part[0],
        later_part[0][:, None, None] * earlier_part[1] + later_part[1],
    )


def backward_merge(earlier_part, later_part):
    return (
        earlier_part[0] * later_part[0],
        later_part[1] + later_part[0][:, None, None] * earlier_part[1],
    )


def run_forward(running, element):
    return (forward_merge(running, element), running)


def run_backward(running, element):
    return (backward_merge(running, element), running)


def select_mine(bundle, inner_pos):
    return tuple(
        (lax.dynamic_index_in_dim(member, inner_pos, 0, keepdims=False) for member in bundle)
    )


def per_device(queries, key_rows, value_rows, out_grad, log_gate):
    row_count = queries.shape[0]
    head_count = log_gate.shape[0]
    head_size = queries.shape[1] // head_count
    devices = lax.axis_size("outer") * lax.axis_size("inner")
    lin_scale = (head_size * row_count * devices) ** (-0.5)
    block_shape = (row_count, head_count, head_size)
    query_blk = queries.reshape(block_shape)
    key_blk = key_rows.reshape(block_shape)
    value_blk = value_rows.reshape(block_shape)
    grad_blk = out_grad.reshape(block_shape)
    block_decay, state_local, grad_local = local_states(
        query_blk, key_blk, value_blk, grad_blk, log_gate
    )
    key_halo, value_halo = from_behind((key_blk[-W:], value_blk[-W:]), ("outer", "inner"), 1)
    position = lax.axis_index("outer") * lax.axis_size("inner") + lax.axis_index("inner")
    identity_pair = (
        jnp.ones((head_count,), jnp.float32),
        jnp.zeros((head_count, head_size, head_size), jnp.float32),
    )
    gathered = (
        lax.all_gather(block_decay[None], "inner", axis=0, tiled=True),
        lax.all_gather(state_local[None], "inner", axis=0, tiled=True),
        lax.all_gather(grad_local[None], "inner", axis=0, tiled=True),
    )
    group_decay, group_state, group_grad = gathered
    total_forward, before_forward = lax.scan(run_forward, identity_pair, (group_decay, group_state))
    total_backward, after_backward = lax.scan(
        run_backward, identity_pair, (group_decay, group_grad), reverse=True
    )
    inner_pos = lax.axis_index("inner")
    mine_forward = select_mine(before_forward, inner_pos)
    mine_backward = select_mine(after_backward, inner_pos)
    outer_forward = carried_in(total_forward, "outer", forward_merge, identity_pair, False)
    outer_backward = carried_in(total_backward, "outer", backward_merge, identity_pair, True)
    forward_pair = forward_merge(outer_forward, mine_forward)
    backward_pair = backward_merge(outer_backward, mine_backward)
    output, query_grad, key_local, value_local, key_back, value_back = block_terms(
        query_blk,
        key_blk,
        value_blk,
        grad_blk,
        log_gate,
        forward_pair[1],
        backward_pair[1],
        key_halo,
        value_halo,
        position > 0,
        lin_scale,
    )
    key_return, value_return = (
        from_behind(key_back.astype(jnp.bfloat16), ("outer", "inner"), -1).astype(key_back.dtype),
        from_behind(value_back.astype(jnp.bfloat16), ("outer", "inner"), -1).astype(
            value_back.dtype
        ),
    )
    key_grad = key_local.at[-W:].add(key_return).astype(jnp.bfloat16)
    value_grad = value_local.at[-W:].add(value_return).astype(jnp.bfloat16)
    flat_shape = (row_count, head_count * head_size)
    return (
        output.reshape(flat_shape),
        query_grad.reshape(flat_shape),
        key_grad.reshape(flat_shape),
        value_grad.reshape(flat_shape),
    )


def solution(mesh):
    placed = (
        P(("outer", "inner"), None),
        P(("outer", "inner"), None),
        P(("outer", "inner"), None),
        P(("outer", "inner"), None),
        P(None, ("outer", "inner")),
    )
    return jax.shard_map(
        per_device,
        mesh=mesh,
        in_specs=placed,
        out_specs=(
            P(("outer", "inner"), None),
            P(("outer", "inner"), None),
            P(("outer", "inner"), None),
            P(("outer", "inner"), None),
        ),
        check_vma=False,
    )
```

profile of v0, /device:TPU:230, one launch (start us, length us, event | category | flops | bytes accessed | tf_op | source)
XLA Modules:
  0.0 660.7 jit_solution(8102679605573216670)
XLA Ops:
  11.1 2.2 fusion.33
  14.6 2.2 fusion.34
  18.4 15.5 %all-reduce = f32[128]{0:T(128)S(1)} all-reduce(f32[128]{0:T(128)S(1)} %dynamic-update-slice.6), channel_id=2, replica_groups=mesh['outer'=32,'inner'=8] {'inner'}, use_global_device_ids=true, to_apply=%add | all-reduce | flops 128 | bytes 1024
  34.0 32.2 %all-gather.16.cloned.1.call-done = f32[128,128,128]{2,1,0:T(8,128)} async-done(((f32[16,128,128]{2,1,0:T(8,128)}), f32[128,128,128]{2,1,0:T(8,128)}) %all-gather.16.cloned.1.call-update) | async-done | bytes 8388624 | tf_op jit(solution)/shard_map/all_gather | solution.py:182
  66.1 4.4 broadcast.104.clone.1
  70.5 21.0 %while.69 = (s32[]{:T(128)}, f32[16]{0:T(128)S(1)}, f32[16,128,128]{2,1,0:T(8,128)S(1)}, f32[8,16]{1,0:T(8,128)S(1)}, f32[8,16,128,128]{3,2,1,0:T(8,128)}, /*ind...) while((s32[]{:T(128)}, f32[16]{0:T(128)S(1)}, ...), condition=%wide.region_9.10_spmd.clone, body=%wide.region_8.9_spmd.clone.sunk | while | flops 1048612 | bytes 5243533 | solution.py:186
  92.6 27.8 %all-gather.12.cloned.1.call-done = f32[128,128,128]{2,1,0:T(8,128)} async-done(((f32[16,128,128]{2,1,0:T(8,128)}), f32[128,128,128]{2,1,0:T(8,128)}) %all-gather.12.cloned.1.call-update) | async-done | bytes 8388624 | tf_op jit(solution)/shard_map/all_gather | solution.py:181
  120.4 4.3 broadcast.104.clone
  124.7 20.6 %while.68 = (s32[]{:T(128)}, f32[16]{0:T(128)S(1)}, f32[16,128,128]{2,1,0:T(8,128)S(1)}, f32[8,16]{1,0:T(8,128)S(1)}, f32[8,16,128,128]{3,2,1,0:T(8,128)}, /*ind...) while((s32[]{:T(128)}, f32[16]{0:T(128)S(1)}, ...), condition=%wide.region_2.3_spmd.clone, body=%wide.region_1.2_spmd.clone.sunk | while | flops 1048611 | bytes 5244021 | solution.py:185
  148.0 2.2 collective-permute-start.1
  151.2 2.5 collective-permute-start
  160.0 2.6 collective-permute-done.1
  162.6 2.7 fusion.70
  165.3 3.3 convolution_bitcast_fusion
  168.6 2.2 slice.107
  170.8 2.5 collective-permute-start.3
  173.3 2.5 fusion.44
  175.8 4.8 convolution_bitcast_fusion.1
  182.8 2.1 collective-permute-start.2
  185.4 72.2 %all-reduce.3 = (f32[512]{0:T(512)S(1)}, f32[512]{0:T(512)S(1)}) all-reduce(f32[512]{0:T(512)S(1)} %dynamic-update-slice.7, f32[512]{0:T(512)S(1)} %dynamic-update-slice.8), channel_id=4, replica_groups=mesh['outer'=32,'inner'=8] {'outer'}, use_global_device_ids=true, to_apply=%add.1 | all-reduce | flops 1024 | bytes 8192
  257.7 100.4 %all-gather.18.cloned.1.call-done = f32[512,128,128]{2,1,0:T(8,128)} async-done(((f32[16,128,128]{2,1,0:T(8,128)}), f32[512,128,128]{2,1,0:T(8,128)}) %all-gather.18.cloned.1.call-update) | async-done | bytes 33554448 | tf_op jit(solution)/shard_map/all_gather | solution.py:19
  358.5 3.3 convolution_bitcast_fusion.4
  363.3 2.4 slice_add_fusion
  365.6 7.0 %scatter-add.9 = f32[128,16,128]{0,2,1:T(8,128)} dynamic-update-slice(f32[128,16,128]{0,2,1:T(8,128)} %copy-done.2, f32[64,16,128]{0,2,1:T(8,128)} %slice_add_fusion, s32[]{:T(128)} %constant.187.clone.1, s32[]{:T(128)} %constant.180.clone.1, s32[]{:T(128)} %constant.180.clone.1) | dynamic-update-slice | bytes 1048580 | tf_op jit(solution)/shard_map/scatter-add | solution.py:216
  375.1 2.8 convolution_bitcast_fusion.5
  379.7 5.1 scatter-add.6
  385.9 204.5 %all-gather.14.cloned.1.call-done = f32[512,128,128]{2,1,0:T(8,128)} async-done(((f32[16,128,128]{2,1,0:T(8,128)}), f32[512,128,128]{2,1,0:T(8,128)}) %all-gather.14.cloned.1.call-update) | async-done | bytes 33554448 | tf_op jit(solution)/shard_map/all_gather | solution.py:19
  590.6 46.6 %while.66 = (s32[]{:T(128)}, f32[16,128,128]{2,1,0:T(8,128)S(1)}, s32[]{:T(128)}, f32[32,16]{1,0:T(8,128)S(1)}, f32[32,16,128,128]{3,2,1,0:T(8,128)}, /*index=5*/s32[]{:T(128)}, s32[]{:T(128)}, s32[]{:T(128)}) while((s32[]{:T(128)}, f32[16,128,128]{2,1,0:T(8,128)S(1)}, s32[]{:T(128)}, f32[32,16]{1,0:T(8,128)S(1)}, ...), condition=%wide.region_4.5_spmd, body=%wide.region_3.4_spmd.sunk | while | flops 524293 | bytes 3146047 | solution.py:28
  637.1 3.6 fusion.20
  640.7 4.3 fusion.26
  646.5 4.2 fusion.22
  650.7 2.5 fusion.25
  (224 shorter events, 115.3 us)
Async XLA Ops:
  7.2 59.0 %all-gather.16.cloned.1.call-start = ((), (), s32[]{:S(2)}) async-start(), calls=%async_computation.2 | async-start | bytes 9437184 | tf_op jit(solution)/shard_map/all_gather | solution.py:182
  11.1 2.3 copy-start.11
  13.3 1.0 copy-start.12
  13.3 107.1 %all-gather.12.cloned.1.call-start = ((), (), s32[]{:S(2)}) async-start(), calls=%async_computation | async-start | bytes 9437184 | tf_op jit(solution)/shard_map/all_gather | solution.py:181
  14.6 2.3 copy-start.17
  16.8 341.3 %all-gather.18.cloned.1.call-start = ((), (), s32[]{:S(2)}) async-start(), calls=%async_computation.3 | async-start | bytes 34603008 | tf_op jit(solution)/shard_map/all_gather | solution.py:19
  91.5 1.0 copy-start
  92.5 498.0 %all-gather.14.cloned.1.call-start = ((), (), s32[]{:S(2)}) async-start(), calls=%async_computation.1 | async-start | bytes 34603008 | tf_op jit(solution)/shard_map/all_gather | solution.py:19
  145.3 1.0 copy-start.1
  146.3 8.1 %copy-start.16 = (u32[256]{0:T(256)S(1)}, u32[256]{0:T(256)}, u32[]{:S(2)}) copy-start(u32[256]{0:T(256)} %constant.203) | copy-start | bytes 3076
  148.0 14.6 %collective-permute-start.1 = (bf16[64,16,128]{2,0,1:T(8,128)(2,1)}, bf16[64,16,128]{2,0,1:T(8,128)(2,1)}, u32[]{:S(2)}, u32[]{:S(2)}) collective-permute-start(bf16[64,16,128]{2,0,1:T(8,128)(2,1)} %copy_bitcast_fusion), channel_id=1, source_target_pairs={{0,1},{1,2},{2,3},{3,4},{4,5},{5,6},{6,7},{7,8},{8,9},{9,10},{10,1... | collective-permute-start | bytes 786440 | tf_op jit(solution)/shard_map/ppermute | solution.py:12
  151.2 22.1 %collective-permute-start = (bf16[64,16,128]{2,0,1:T(8,128)(2,1)S(1)}, bf16[64,16,128]{2,0,1:T(8,128)(2,1)}, u32[]{:S(2)}, u32[]{:S(2)}) collective-permute-start(bf16[64,16,128]{2,0,1:T(8,128)(2,1)S(1)} %copy_bitcast_fusion.1), channel_id=1, source_target_pairs={{0,1},{1,2},{2,3},{3,4},{4,5},{5,6},{6,7},{7,8},{8,9},{9,10},{10,1... | collective-permute-start | bytes 786440 | tf_op jit(solution)/shard_map/ppermute | solution.py:12
  154.0 11.2 %copy-start.15 = (bf16[128,16,128]{2,0,1:T(8,128)(2,1)}, bf16[128,16,128]{2,0,1:T(8,128)(2,1)S(1)}, u32[]{:S(2)}) copy-start(bf16[128,16,128]{2,0,1:T(8,128)(2,1)S(1)} %copy.84) | copy-start | bytes 1572868
  154.3 19.0 %copy-start.5 = (bf16[128,16,128]{2,0,1:T(8,128)(2,1)}, bf16[128,16,128]{2,0,1:T(8,128)(2,1)S(1)}, u32[]{:S(2)}) copy-start(bf16[128,16,128]{2,0,1:T(8,128)(2,1)S(1)} %copy.82) | copy-start | bytes 1572868
  156.4 2.1 copy-start.9
  157.0 3.0 copy-start.7
  170.8 191.5 %collective-permute-start.3 = (bf16[64,16,128]{0,2,1:T(8,128)(2,1)}, bf16[64,16,128]{0,2,1:T(8,128)(2,1)}, u32[]{:S(2)}, u32[]{:S(2)}) collective-permute-start(bf16[64,16,128]{0,2,1:T(8,128)(2,1)} %slice.107), channel_id=1, source_target_pairs={{1,0},{2,1},{3,2},{4,3},{5,4},{6,5},{7,6},{8,7},{9,8},{10,9},{11,1... | collective-permute-start | bytes 786440 | tf_op jit(solution)/shard_map/ppermute | solution.py:12
  182.8 195.6 %collective-permute-start.2 = (bf16[64,16,128]{0,2,1:T(8,128)(2,1)}, bf16[64,16,128]{0,2,1:T(8,128)(2,1)}, u32[]{:S(2)}, u32[]{:S(2)}) collective-permute-start(bf16[64,16,128]{0,2,1:T(8,128)(2,1)} %slice.108), channel_id=1, source_target_pairs={{1,0},{2,1},{3,2},{4,3},{5,4},{6,5},{7,6},{8,7},{9,8},{10,9},{11,1... | collective-permute-start | bytes 786440 | tf_op jit(solution)/shard_map/ppermute | solution.py:12
  358.5 3.4 copy-start.10
  358.5 3.4 copy-start.14
  362.3 1.0 copy-start.2
  375.1 2.8 copy-start.8
  375.1 2.8 copy-start.13
  590.6 46.6 %copy-start.4 = (f32[128,16,128]{0,2,1:T(8,128)S(1)}, f32[128,16,128]{0,2,1:T(8,128)}, u32[]{:S(2)}) copy-start(f32[128,16,128]{0,2,1:T(8,128)} %convolution_bitcast_fusion.7) | copy-start | bytes 3145732
  645.0 1.4 copy-start.3
  646.5 4.2 copy-start.6
Sparse Core Ops, SparseCore 0:
  13.5 52.6 all-gather.15
  68.0 52.3 all-gather.11
  123.0 235.1 all-gather.17
  360.6 229.8 all-gather.13
where the time goes:
time: 664 us; the launch traced here: 661 us
  waiting for transfers between devices  368 us (55%)
  other arithmetic  92.1 us (14%)
  blocking collectives  87.6 us (13%)
  matrix products  43.3 us (7%)
  local copies, waits for them, and re-layouts  43.1 us (6%)
  between operations  15.6 us (2%)
  starting transfers between devices  9.56 us (1%)
    all_gather x2, waiting for transfers between devices, carried_in(): gathered = jax.tree.map(lambda a: lax.all_gather(a, axis), part)  305 us
    unnamed x2, blocking collectives  87.6 us
    add x39, other arithmetic, forward_merge(): later_part[0][:, None, None] * earlier_part[1] + later_part[1]  56.4 us
    all_gather x1, waiting for transfers between devices, per_device(): lax.all_gather(grad_local[None], 'inner', axis=0, tiled=True)  32.2 us
    all_gather x1, waiting for transfers between devices, per_device(): lax.all_gather(state_local[None], 'inner', axis=0, tiled=True)  27.8 us
    dot_general x11, matrix products, low_product(): return jnp.einsum(form, left, right, preferred_element_type=jnp.float32)  22.3 us
    dot_general x6, matrix products, high_product(): return jnp.einsum(form, left, right, precision=lax.Precision.HIGHEST)  18.3 us
    dynamic_update_slice x16, other arithmetic, per_device(): lax.scan(run_forward, identity_pair, (group_decay, group_state))  17.3 us
  transfers between devices with their start and end apart: 8, of which 5 were waited for; matrix products, arithmetic and copies ran while one was open for 16% of the time, Pallas kernels for 0%

commit v1 on v0

--- a/solution.py
+++ b/solution.py
@@ -4,6 +4,13 @@
 from jax.sharding import PartitionSpec as P
 
 W = 64
+
+
+def lead_frame(w_in):
+    g_now = lax.axis_size("inner")
+    b_now = jnp.stack(g_now * [w_in], axis=0)
+    k_now = lax.all_to_all(b_now, axis_name="inner", split_axis=0, concat_axis=0)
+    return jnp.concatenate(k_now, axis=0)
 
 
 def from_behind(value, axis, steps):
@@ -179,7 +186,7 @@
     gathered = (
         lax.all_gather(block_decay[None], "inner", axis=0, tiled=True),
         lax.all_gather(state_local[None], "inner", axis=0, tiled=True),
-        lax.all_gather(grad_local[None], "inner", axis=0, tiled=True),
+        lead_frame(grad_local[None]),
     )
     group_decay, group_state, group_grad = gathered
     total_forward, before_forward = lax.scan(run_forward, identity_pair, (group_decay, group_state))

time: 664 us -> 728 us (1.096)
  blocking collectives: 87.6 us -> 207 us
  waiting for transfers between devices: 368 us -> 300 us
  starting transfers between devices: 9.56 us -> 17.3 us
    unnamed x2, blocking collectives: 87.6 us -> 207 us
    all_gather x1 -> x0, waiting for transfers between devices: 32.2 us -> none  [per_device(): lax.all_gather(grad_local[None], 'inner', axis=0, tiled=True)]
    all_gather x1, waiting for transfers between devices: 27.8 us -> 0.02 us  [per_device(): lax.all_gather(state_local[None], 'inner', axis=0, tiled=True)]
  transfers between devices with their start and end apart: 8 -> 8, of which waited for: 5 -> 2; matrix products, arithmetic and copies ran while one was open for 16% -> 15% of each run, Pallas kernels for 0% -> 0%
where the time goes in v1:
time: 728 us; the launch traced here: 724 us
  waiting for transfers between devices  300 us (41%)
  blocking collectives  207 us (28%)
  other arithmetic  92.1 us (13%)
  local copies, waits for them, and re-layouts  48.3 us (7%)
  matrix products  42.5 us (6%)
  starting transfers between devices  17.3 us (2%)
  between operations  15.6 us (2%)
    all_gather x2, waiting for transfers between devices, carried_in(): gathered = jax.tree.map(lambda a: lax.all_gather(a, axis), part)  300 us
    unnamed x2, blocking collectives  207 us
    add x39, other arithmetic, forward_merge(): later_part[0][:, None, None] * earlier_part[1] + later_part[1]  56.6 us
    dot_general x11, matrix products, low_product(): return jnp.einsum(form, left, right, preferred_element_type=jnp.float32)  22.4 us
    dynamic_update_slice x16, other arithmetic, per_device(): lax.scan(run_forward, identity_pair, (group_decay, group_state))  17.3 us
    dot_general x6, matrix products, high_product(): return jnp.einsum(form, left, right, precision=lax.Precision.HIGHEST)  17.3 us
  transfers between devices with their start and end apart: 8, of which 2 were waited for; matrix products, arithmetic and copies ran while one was open for 15% of the time, Pallas kernels for 0%

profile of v1, /device:TPU:230, one launch (start us, length us, event | category | flops | bytes accessed | tf_op | source)
XLA Modules:
  0.0 724.5 jit_solution(6350064936128534855)
XLA Ops:
  11.1 2.3 fusion.34
  15.9 4.3 stack.3
  20.2 5.2 all-to-all-start
  27.0 131.6 %all-reduce = f32[128]{0:T(128)S(1)} all-reduce(f32[128]{0:T(128)S(1)} %dynamic-update-slice.6), channel_id=2, replica_groups=mesh['outer'=32,'inner'=8] {'inner'}, use_global_device_ids=true, to_apply=%add | all-reduce | flops 128 | bytes 1024
  158.6 4.4 broadcast.106.clone.1
  163.0 20.7 %while.69 = (s32[]{:T(128)}, f32[16]{0:T(128)S(1)}, f32[16,128,128]{2,1,0:T(8,128)S(1)}, f32[8,16]{1,0:T(8,128)S(1)}, f32[8,16,128,128]{3,2,1,0:T(8,128)}, /*ind...) while((s32[]{:T(128)}, f32[16]{0:T(128)S(1)}, ...), condition=%wide.region_9.10_spmd.clone, body=%wide.region_8.9_spmd.clone.sunk | while | flops 1048612 | bytes 5243533 | solution.py:193
  184.8 4.3 broadcast.106.clone
  189.1 20.8 %while.68 = (s32[]{:T(128)}, f32[16]{0:T(128)S(1)}, f32[16,128,128]{2,1,0:T(8,128)S(1)}, f32[8,16]{1,0:T(8,128)S(1)}, f32[8,16,128,128]{3,2,1,0:T(8,128)}, /*ind...) while((s32[]{:T(128)}, f32[16]{0:T(128)S(1)}, ...), condition=%wide.region_2.3_spmd.clone, body=%wide.region_1.2_spmd.clone.sunk | while | flops 1048611 | bytes 5244021 | solution.py:192
  211.0 1.7 copy_bitcast_fusion
  212.7 1.9 collective-permute-start.1
  215.6 3.0 collective-permute-start
  225.6 2.9 fusion.70
  228.5 3.3 convolution_bitcast_fusion
  231.8 2.2 slice.107
  234.0 4.7 collective-permute-start.3
  238.7 2.5 fusion.44
  241.2 4.8 convolution_bitcast_fusion.1
  246.0 2.1 slice.108
  248.1 2.4 collective-permute-start.2
  251.1 75.5 %all-reduce.3 = (f32[512]{0:T(512)S(1)}, f32[512]{0:T(512)S(1)}) all-reduce(f32[512]{0:T(512)S(1)} %dynamic-update-slice.7, f32[512]{0:T(512)S(1)} %dynamic-update-slice.8), channel_id=4, replica_groups=mesh['outer'=32,'inner'=8] {'outer'}, use_global_device_ids=true, to_apply=%add.1 | all-reduce | flops 1024 | bytes 8192
  326.8 95.9 %all-gather.14.cloned.1.call-done = f32[512,128,128]{2,1,0:T(8,128)} async-done(((f32[16,128,128]{2,1,0:T(8,128)}), f32[512,128,128]{2,1,0:T(8,128)}) %all-gather.14.cloned.1.call-update) | async-done | bytes 33554448 | tf_op jit(solution)/shard_map/all_gather | solution.py:26
  423.0 3.3 convolution_bitcast_fusion.4
  427.8 2.4 slice_add_fusion
  430.2 7.0 scatter-add.9
  439.7 2.7 convolution_bitcast_fusion.5
  444.1 5.1 scatter-add.6
  450.4 203.7 %all-gather.12.cloned.1.call-done = f32[512,128,128]{2,1,0:T(8,128)} async-done(((f32[16,128,128]{2,1,0:T(8,128)}), f32[512,128,128]{2,1,0:T(8,128)}) %all-gather.12.cloned.1.call-update) | async-done | bytes 33554448 | tf_op jit(solution)/shard_map/all_gather | solution.py:26
  654.1 46.8 %while.66 = (s32[]{:T(128)}, f32[16,128,128]{2,1,0:T(8,128)S(1)}, s32[]{:T(128)}, f32[32,16]{1,0:T(8,128)S(1)}, f32[32,16,128,128]{3,2,1,0:T(8,128)}, /*index=5*/s32[]{:T(128)}, s32[]{:T(128)}, s32[]{:T(128)}) while((s32[]{:T(128)}, f32[16,128,128]{2,1,0:T(8,128)S(1)}, s32[]{:T(128)}, f32[32,16]{1,0:T(8,128)S(1)}, ...), condition=%wide.region_4.5_spmd, body=%wide.region_3.4_spmd.sunk | while | flops 524293 | bytes 3146047 | solution.py:35
  700.9 3.6 fusion.20
  704.5 4.3 fusion.26
  710.2 4.2 fusion.22
  714.5 2.5 fusion.25
  (224 shorter events, 113.5 us)
Async XLA Ops:
  7.2 177.6 %all-gather.10.cloned.1.call-start = ((), (), s32[]{:S(2)}) async-start(), calls=%async_computation.1 | async-start | bytes 9437184 | tf_op jit(solution)/shard_map/all_gather | solution.py:188
  11.1 2.3 copy-start.13
  13.4 1.0 copy-start.14
  20.2 5.3 copy-start.17
  20.2 138.4 %all-to-all-start = ((f32[8,1,16,128,128]{4,3,2,1,0:T(8,128)}), f32[8,1,16,128,128]{4,3,2,1,0:T(8,128)}, u32[]{:S(2)}, u32[]{:S(2)}) async-start(f32[8,1,16,128,128]{4,3,2,1,0:T(8,128)} %stack.3), calls=%async_computation | async-start | bytes 16777216 | tf_op jit(solution)/shard_map/all_to_all | solution.py:12
  25.4 397.3 %all-gather.14.cloned.1.call-start = ((), (), s32[]{:S(2)}) async-start(), calls=%async_computation.3 | async-start | bytes 34603008 | tf_op jit(solution)/shard_map/all_gather | solution.py:26
  183.7 1.0 copy-start
  184.7 469.3 %all-gather.12.cloned.1.call-start = ((), (), s32[]{:S(2)}) async-start(), calls=%async_computation.2 | async-start | bytes 34603008 | tf_op jit(solution)/shard_map/all_gather | solution.py:26
  210.0 1.0 copy-start.1
  211.0 9.0 %copy-start.16 = (u32[256]{0:T(256)S(1)}, u32[256]{0:T(256)}, u32[]{:S(2)}) copy-start(u32[256]{0:T(256)} %constant.203) | copy-start | bytes 3076
  212.7 12.9 %collective-permute-start.1 = (bf16[64,16,128]{2,0,1:T(8,128)(2,1)}, bf16[64,16,128]{2,0,1:T(8,128)(2,1)}, u32[]{:S(2)}, u32[]{:S(2)}) collective-permute-start(bf16[64,16,128]{2,0,1:T(8,128)(2,1)} %copy_bitcast_fusion), channel_id=1, source_target_pairs={{0,1},{1,2},{2,3},{3,4},{4,5},{5,6},{6,7},{7,8},{8,9},{9,10},{10,1... | collective-permute-start | bytes 786440 | tf_op jit(solution)/shard_map/ppermute | solution.py:19
  215.6 23.1 %collective-permute-start = (bf16[64,16,128]{2,0,1:T(8,128)(2,1)S(1)}, bf16[64,16,128]{2,0,1:T(8,128)(2,1)}, u32[]{:S(2)}, u32[]{:S(2)}) collective-permute-start(bf16[64,16,128]{2,0,1:T(8,128)(2,1)S(1)} %copy_bitcast_fusion.1), channel_id=1, source_target_pairs={{0,1},{1,2},{2,3},{3,4},{4,5},{5,6},{6,7},{7,8},{8,9},{9,10},{10,1... | collective-permute-start | bytes 786440 | tf_op jit(solution)/shard_map/ppermute | solution.py:19
  219.9 18.8 %copy-start.5 = (bf16[128,16,128]{2,0,1:T(8,128)(2,1)}, bf16[128,16,128]{2,0,1:T(8,128)(2,1)S(1)}, u32[]{:S(2)}) copy-start(bf16[128,16,128]{2,0,1:T(8,128)(2,1)S(1)} %copy.82) | copy-start | bytes 1572868
  222.0 2.1 copy-start.9
  222.5 3.1 copy-start.7
  225.6 2.9 copy-start.15
  234.0 192.8 %collective-permute-start.3 = (bf16[64,16,128]{0,2,1:T(8,128)(2,1)}, bf16[64,16,128]{0,2,1:T(8,128)(2,1)}, u32[]{:S(2)}, u32[]{:S(2)}) collective-permute-start(bf16[64,16,128]{0,2,1:T(8,128)(2,1)} %slice.107), channel_id=1, source_target_pairs={{1,0},{2,1},{3,2},{4,3},{5,4},{6,5},{7,6},{8,7},{9,8},{10,9},{11,1... | collective-permute-start | bytes 786440 | tf_op jit(solution)/shard_map/ppermute | solution.py:19
  248.1 194.6 %collective-permute-start.2 = (bf16[64,16,128]{0,2,1:T(8,128)(2,1)}, bf16[64,16,128]{0,2,1:T(8,128)(2,1)}, u32[]{:S(2)}, u32[]{:S(2)}) collective-permute-start(bf16[64,16,128]{0,2,1:T(8,128)(2,1)} %slice.108), channel_id=1, source_target_pairs={{1,0},{2,1},{3,2},{4,3},{5,4},{6,5},{7,6},{8,7},{9,8},{10,9},{11,1... | collective-permute-start | bytes 786440 | tf_op jit(solution)/shard_map/ppermute | solution.py:19
  423.0 3.4 copy-start.10
  423.0 3.4 copy-start.12
  426.8 1.0 copy-start.2
  439.7 2.7 copy-start.8
  439.7 2.7 copy-start.11
  654.1 46.8 %copy-start.4 = (f32[128,16,128]{0,2,1:T(8,128)S(1)}, f32[128,16,128]{0,2,1:T(8,128)}, u32[]{:S(2)}) copy-start(f32[128,16,128]{0,2,1:T(8,128)} %convolution_bitcast_fusion.7) | copy-start | bytes 3145732
  708.8 1.4 copy-start.3
  710.2 4.2 copy-start.6
Sparse Core Ops, SparseCore 0:
  13.5 96.9 all-gather.9
  184.8 237.7 all-gather.13
  425.3 228.7 all-gather.11
